TPU v7x, 32 devices: a whole 2x2x4 slice. The times are simulated.
32 devices in a mesh: dp: 2 (over y), fsdp: 16 (over z, x, core).
Axes of the slice: x: 2, y: 2, z: 4, core: 2. Of those that a mesh axis runs over, the one named last changes fastest.
Arguments:
- ids: int32 [2, 192], P('dp'), may hold values from 0 to 511
- embed: bfloat16 [512, 8192], P(None, 'fsdp'), may hold values from -32 to 32
- gain: bfloat16 [8192], P('fsdp'), may hold values from 0.099609375 to 1.8984375
- w_in: bfloat16 [3, 4096, 8192], P(None, 'fsdp'), may hold values from -0.0625 to 0.0625
- feat_filter: float32 [3, 256, 7], P(None, 'fsdp'), may hold values from -2.4 to 2.4
- inner_filter: float32 [256, 7], P('fsdp'), may hold values from -2.4 to 2.4
- w_out: bfloat16 [4096, 8192], P(None, 'fsdp'), may hold values from -0.09375 to 0.09375
- cotangent: bfloat16 [2, 192, 8192], P('dp', None, 'fsdp'), may hold values from -6 to 6
- right_prev: bfloat16 [8192, 256], P('fsdp'), may hold values from -6 to 6
Outputs:
- block_out: bfloat16 [2, 192, 8192], P('dp', None, 'fsdp')
- filter_grad: float32 [4, 256, 7], P(None, 'fsdp')
- basis: bfloat16 [4096, 256], P('fsdp')
- right_factor: float32 [8192, 256], P('fsdp')
All inputs are finite; a program needn't handle non-finite values.
Results may differ from a plain program's by a relative error of at most 0.014.
The roundings to bfloat16 on the way count: a program that leaves them out, or rounds other values in their place, can miss the bound.
Values may be sent and summed in bfloat16 or wider, within the bound.
No kernel may reach another device: no remote copies, remote signals or barrier semaphores. Data moves between devices by JAX's collectives and lax.ppermute only.
A program may use at most 128 MiB of HBM per device.

v0:
```python
import jax
import jax.numpy as jnp
from jax import lax
from jax.sharding import PartitionSpec as P

D = 8192
C = 4096
GROUP = 16


def shifted(signal, lag, tap_count):
    padded = jnp.pad(signal, ((tap_count - 1, 0), (0, 0)))
    first = tap_count - 1 - lag
    return padded[first : first + signal.shape[0]]


def causal(signal, tap_table):
    tap_count = tap_table.shape[0]
    result = jnp.zeros(signal.shape, jnp.float32)
    for lag in range(tap_count):
        result = result + tap_table[lag][None, :] * shifted(signal, lag, tap_count)
    return result


def anticausal(signal, tap_table):
    tap_count = tap_table.shape[0]
    padded = jnp.pad(signal, ((0, tap_count - 1), (0, 0)))
    result = jnp.zeros(signal.shape, jnp.float32)
    for lag in range(tap_count):
        result = result + tap_table[lag][None, :] * padded[lag : lag + signal.shape[0]]
    return result


def tap_sums(gradient, signal, tap_count):
    listing = []
    for lag in range(tap_count):
        listing.append(jnp.sum(gradient * shifted(signal, lag, tap_count), axis=0))
    stacked = jnp.stack(listing, axis=0)
    grouped = stacked.reshape(tap_count, stacked.shape[1] // GROUP, GROUP).sum(axis=2)
    return grouped.T


def expand(filters):
    return jnp.repeat(filters.T, GROUP, axis=1)


def per_device(ids, embed, gain, w_in, feat_filter, inner_filter, w_out, cotangent, right_prev):
    tokens = ids[0]
    length = tokens.shape[0]
    tap_count = inner_filter.shape[1]
    onehot = (tokens[:, None] == jnp.arange(embed.shape[0], dtype=jnp.int32)[None, :]).astype(
        jnp.bfloat16
    )
    x_cols = jnp.dot(onehot, embed, preferred_element_type=jnp.float32)
    square_sums = lax.psum(jnp.sum(x_cols * x_cols, axis=1), "fsdp")
    factor = lax.rsqrt(square_sums / D + 1e-05)
    normed_cols = (x_cols * factor[:, None] * gain.astype(jnp.float32)[None, :]).astype(
        jnp.bfloat16
    )
    projected = jnp.einsum(
        "ld,kcd->klc",
        lax.all_gather(normed_cols, "fsdp", axis=1, tiled=True),
        w_in,
        preferred_element_type=jnp.float32,
    )
    rounded = lax.optimization_barrier(projected.astype(jnp.bfloat16)).astype(jnp.float32)
    query, key_in, value = (rounded[0], rounded[1], rounded[2])
    query_conv = causal(query, expand(feat_filter[0]))
    key_conv = causal(key_in, expand(feat_filter[1]))
    value_conv = causal(value, expand(feat_filter[2]))
    gated = key_conv * value_conv
    inner_table = expand(inner_filter)
    window = causal(gated, inner_table)
    gated_out = (query_conv * window).astype(jnp.bfloat16)
    cot_cols = cotangent[0]
    shard_piece = lax.all_gather(gated_out, "fsdp", axis=1, tiled=True)
    weight_rows = w_out
    mixed_sum = jnp.dot(shard_piece, weight_rows, preferred_element_type=jnp.float32)
    term = jnp.einsum("lc,ld->cd", shard_piece, cot_cols, preferred_element_type=jnp.float32)
    mixed_sum, grad_part = (mixed_sum, term)
    block_out = (x_cols + mixed_sum).astype(jnp.bfloat16)[None]
    weight_rows = w_out
    mixed_grad = lax.psum_scatter(
        jnp.einsum("cd,ld->cl", weight_rows, cot_cols, preferred_element_type=jnp.float32),
        "fsdp",
        scatter_dimension=0,
        tiled=True,
    ).T
    query_grad = mixed_grad * window
    window_grad = mixed_grad * query_conv
    gated_grad = anticausal(window_grad, inner_table)
    key_grad = gated_grad * value_conv
    value_grad = gated_grad * key_conv
    norm_factor = 1.0 / jnp.sqrt(jnp.float32(lax.axis_size("dp") * length))
    filter_part = (
        jnp.stack(
            [
                tap_sums(query_grad, query, tap_count),
                tap_sums(key_grad, key_in, tap_count),
                tap_sums(value_grad, value, tap_count),
                tap_sums(window_grad, gated, tap_count),
            ],
            axis=0,
        )
        * norm_factor
    )
    grad_total, filter_grad = (
        lax.psum(grad_part.astype(jnp.bfloat16), "dp").astype(jnp.float32),
        lax.psum(filter_part.astype(jnp.bfloat16), "dp").astype(jnp.float32),
    )
    grad_half = grad_total.astype(jnp.bfloat16)
    grad_rows_own = lax.all_to_all(grad_half, "fsdp", split_axis=0, concat_axis=1, tiled=True)
    panel_own = jnp.dot(
        grad_rows_own,
        lax.all_gather(right_prev, "fsdp", axis=0, tiled=True),
        preferred_element_type=jnp.float32,
    ).astype(jnp.bfloat16)
    root_scale = jnp.sqrt(jnp.float32(C))
    gram_local = jnp.einsum("cr,cs->rs", panel_own, panel_own, preferred_element_type=jnp.float32)
    gram_matrix = lax.psum(gram_local, "fsdp")
    lower_factor = jnp.linalg.cholesky(gram_matrix)
    solved = jax.scipy.linalg.solve_triangular(
        lower_factor, panel_own.astype(jnp.float32).T, lower=True
    ).T
    basis_own = (solved * root_scale).astype(jnp.bfloat16)
    right_raw = jnp.einsum(
        "cd,cr->dr",
        grad_half,
        lax.all_gather(basis_own, "fsdp", axis=0, tiled=True),
        preferred_element_type=jnp.float32,
    )
    column_sums = lax.psum(jnp.sum(right_raw * right_raw, axis=0), "fsdp")
    right_factor = right_raw * lax.rsqrt(column_sums / D + 1e-06)[None, :]
    return (block_out, filter_grad, basis_own, right_factor)


def solution(mesh):
    placed = (
        P("dp", None),
        P(None, "fsdp"),
        P("fsdp"),
        P(None, "fsdp", None),
        P(None, "fsdp", None),
        P("fsdp", None),
        P(None, "fsdp"),
        P("dp", None, "fsdp"),
        P("fsdp", None),
    )
    return jax.shard_map(
        per_device,
        mesh=mesh,
        in_specs=placed,
        out_specs=(P("dp", None, "fsdp"), P(None, "fsdp", None), P("fsdp", None), P("fsdp", None)),
        check_vma=False,
    )
```

profile of v0, /device:TPU:0, one launch (start us, length us, event | category | flops | bytes accessed | tf_op | source)
XLA Modules:
  0.0 699.4 jit_solution(17935779332028869934)
XLA Ops:
  9.3 34.9 %psum.35 = f32[192]{0:T(256)S(1)} all-reduce(f32[192]{0:T(256)S(1)} %get-tuple-element.121), channel_id=1, replica_groups=mesh['dp'=2,'fsdp'=16] {'fsdp'}, use_global_device_ids=true, to_apply=%region_1.0 | all-reduce | flops 192 | bytes 1536 | tf_op jit(solution)/shard_map/psum | solution.py:55
  45.1 5.4 fusion.14
  55.0 34.7 %all-gather.5.cloned.1.call-done = bf16[192,8192]{1,0:T(8,128)(2,1)} async-done(((bf16[192,512]{1,0:T(8,128)(2,1)}), bf16[192,8192]{1,0:T(8,128)(2,1)}) %all-gather.5.cloned.1.call-update) | async-done | bytes 3145744 | tf_op jit(solution)/shard_map/all_gather | solution.py:62
  89.7 9.8 %fusion.6 = bf16[3,192,256]{2,1,0:T(8,128)(2,1)S(1)} fusion(bf16[3,256,8192]{2,1,0:T(8,128)(2,1)} %param.12, bf16[192,8192]{1,0:T(8,128)(2,1)} %all-gather.5.cloned.1.call-done), kind=kOutput, calls=%fused_computation.8 | convolution fusion | flops 2416066560 | bytes 16023552 | tf_op jit(solution)/shard_map/ld,kcd->klc/dot_general | solution.py:60
  99.6 58.3 %reduce-scatter.2.cloned.1.call-done = f32[256,192]{0,1:T(8,128)} async-done(((f32[4096,192]{0,1:T(8,128)}), f32[256,192]{0,1:T(8,128)}) %reduce-scatter.2.cloned.1.call-update) | async-done | bytes 196624 | tf_op jit(solution)/shard_map/reduce_scatter | solution.py:83
  164.3 38.0 %all-gather.7.cloned.1.call-done = bf16[192,4096]{1,0:T(8,128)(2,1)} async-done(((bf16[192,256]{1,0:T(8,128)(2,1)}), bf16[192,4096]{1,0:T(8,128)(2,1)}) %all-gather.7.cloned.1.call-update) | async-done | bytes 1572880 | tf_op jit(solution)/shard_map/all_gather | solution.py:76
  202.3 4.7 convolution_convert_fusion
  207.7 106.5 %all-reduce.9.cloned.1.call-done = bf16[4096,512]{1,0:T(8,128)(2,1)} async-done(((bf16[4096,512]{1,0:T(8,128)(2,1)}), bf16[4096,512]{1,0:T(8,128)(2,1)}) %all-reduce.9.cloned.1.call-update) | async-done | bytes 4194320 | tf_op jit(solution)/shard_map/psum | solution.py:108
  314.2 6.4 copy.22
  320.6 5.7 all-to-all-start
  326.3 94.7 %all-gather.9.cloned.1.call-done = bf16[8192,256]{1,0:T(8,128)(2,1)} async-done(((bf16[512,256]{1,0:T(8,128)(2,1)}), bf16[8192,256]{1,0:T(8,128)(2,1)}) %all-gather.9.cloned.1.call-update) | async-done | bytes 4194320 | tf_op jit(solution)/shard_map/all_gather | solution.py:115
  421.0 6.5 all-to-all-done
  427.4 4.8 convolution_convert_fusion.1
  434.0 103.0 %all-reduce.11.cloned.1.call-done = f32[256,256]{0,1:T(8,128)} async-done(((f32[256,256]{0,1:T(8,128)}), f32[256,256]{0,1:T(8,128)}) %all-reduce.11.cloned.1.call-update) | async-done | bytes 262160 | tf_op jit(solution)/shard_map/psum | solution.py:120
  540.6 11.7 %cholesky.50 = f32[128,128]{1,0:T(8,128)S(1)} custom-call(f32[128,128]{1,0:T(8,128)S(1)} %cholesky.118), custom_call_target="Cholesky" | custom-call | tf_op jit(solution)/shard_map/jit(cholesky)/cholesky | solution.py:121
  553.6 9.8 %custom-call.15 = f32[1,128,128]{1,2,0:T(8,128)S(1)} custom-call(f32[1,128,128]{2,1,0:T(8,128)S(1)} %get-tuple-element.89), custom_call_target="InvertDiagBlocksLowerTriangular" | custom-call | tf_op jit(solution)/shard_map/jit(cholesky)/cholesky | solution.py:121
  566.2 11.7 %cholesky.105 = f32[128,128]{1,0:T(8,128)S(1)} custom-call(f32[128,128]{1,0:T(8,128)S(1)} %convolution_subtract_fusion.1), custom_call_target="Cholesky" | custom-call | tf_op jit(solution)/shard_map/jit(cholesky)/cholesky | solution.py:121
  584.2 6.8 while.1
  591.0 20.5 %custom-call.16 = f32[2,128,128]{1,2,0:T(8,128)S(1)} custom-call(f32[2,128,128]{2,1,0:T(8,128)} %get-tuple-element.11), custom_call_target="InvertDiagBlocksLowerTriangular" | custom-call | tf_op jit(solution)/shard_map/jit(_solve_triangular)/triangular_solve | solution.py:122
  622.1 5.0 psum.36
  627.8 3.8 fusion.9
  632.4 23.5 %all-gather.11.cloned.1.call-done = bf16[4096,256]{0,1:T(8,128)(2,1)} async-done(((bf16[256,256]{0,1:T(8,128)(2,1)}), bf16[4096,256]{0,1:T(8,128)(2,1)}) %all-gather.11.cloned.1.call-update) | async-done | bytes 2097168 | tf_op jit(solution)/shard_map/all_gather | solution.py:129
  655.9 4.2 multiply_reduce_fusion
  660.1 31.6 %psum.39 = f32[256]{0:T(256)S(1)} all-reduce(f32[256]{0:T(256)S(1)} %get-tuple-element.125), channel_id=1, replica_groups=mesh['dp'=2,'fsdp'=16] {'fsdp'}, use_global_device_ids=true, to_apply=%region_43.44 | all-reduce | flops 256 | bytes 2048 | tf_op jit(solution)/shard_map/psum | solution.py:132
  (198 shorter events, 48.3 us)
Async XLA Ops:
  7.2 1.1 copy-start
  7.2 82.5 %all-gather.5.cloned.1.call-start = ((), (), s32[]{:S(2)}) async-start(), calls=%async_computation.2 | async-start | bytes 3342336 | tf_op jit(solution)/shard_map/all_gather | solution.py:62
  45.0 5.5 copy-start.8
  45.0 6.6 copy-start.9
  45.1 112.9 %reduce-scatter.2.cloned.1.call-start = ((), (), s32[]{:S(2)}) async-start(), calls=%async_computation.4 | async-start | bytes 3342336 | tf_op jit(solution)/shard_map/reduce_scatter | solution.py:83
  50.5 151.8 %all-gather.7.cloned.1.call-start = ((), (), s32[]{:S(2)}) async-start(), calls=%async_computation.3 | async-start | bytes 1671168 | tf_op jit(solution)/shard_map/all_gather | solution.py:76
  99.5 102.8 %copy-start.7 = (bf16[1,192,512]{2,1,0:T(8,128)(2,1)S(1)}, bf16[1,192,512]{2,1,0:T(8,128)(2,1)}, u32[]{:S(2)}) copy-start(bf16[1,192,512]{2,1,0:T(8,128)(2,1)} %param.16) | copy-start | bytes 589828
  99.6 61.3 %copy-start.3 = (f32[192,256]{1,0:T(8,128)}, f32[192,256]{1,0:T(8,128)S(1)}, u32[]{:S(2)}) copy-start(f32[192,256]{1,0:T(8,128)S(1)} %get-tuple-element.84) | copy-start | bytes 589828
  159.1 48.0 %copy-start.4 = (f32[192,256]{1,0:T(8,128)}, f32[192,256]{1,0:T(8,128)S(1)}, u32[]{:S(2)}) copy-start(f32[192,256]{1,0:T(8,128)S(1)} %get-tuple-element.79) | copy-start | bytes 589828
  161.0 46.1 %copy-start.2 = (f32[192,256]{1,0:T(8,128)}, f32[192,256]{1,0:T(8,128)S(1)}, u32[]{:S(2)}) copy-start(f32[192,256]{1,0:T(8,128)S(1)} %mul.459) | copy-start | bytes 589828
  164.2 150.0 %all-reduce.9.cloned.1.call-start = ((), (), s32[]{:S(2)}) async-start(), calls=%async_computation.5 | async-start | bytes 8388608 | tf_op jit(solution)/shard_map/psum | solution.py:108
  207.1 213.9 %all-gather.9.cloned.1.call-start = ((), (), s32[]{:S(2)}) async-start(), calls=%async_computation.6 | async-start | bytes 4456448 | tf_op jit(solution)/shard_map/all_gather | solution.py:115
  320.6 106.8 %all-to-all-start = ((bf16[16,256,512]{1,2,0:T(8,128)(2,1)}), bf16[16,256,512]{1,2,0:T(8,128)(2,1)}, u32[]{:S(2)}, u32[]{:S(2)}) async-start(bf16[16,256,512]{1,2,0:T(8,128)(2,1)} %copy.22), calls=%async_computation.1 | async-start | bytes 8388608 | tf_op jit(solution)/shard_map/all_to_all | solution.py:112
  326.2 210.8 %all-reduce.11.cloned.1.call-start = ((), (), s32[]{:S(2)}) async-start(), calls=%async_computation.7 | async-start | bytes 524288 | tf_op jit(solution)/shard_map/psum | solution.py:120
  433.2 222.7 %all-gather.11.cloned.1.call-start = ((), (), s32[]{:S(2)}) async-start(), calls=%async_computation.8 | async-start | bytes 2228224 | tf_op jit(solution)/shard_map/all_gather | solution.py:129
  434.0 193.8 %copy-start.1 = (bf16[192,4096]{1,0:T(8,128)(2,1)S(1)}, bf16[192,4096]{1,0:T(8,128)(2,1)}, u32[]{:S(2)}) copy-start(bf16[192,4096]{1,0:T(8,128)(2,1)} %all-gather.7.cloned.1.call-done) | copy-start | bytes 4718596
  539.9 0.7 copy-start.6
  616.6 15.0 %copy-start.5 = (bf16[256,256]{0,1:T(8,128)(2,1)S(1)}, bf16[256,256]{0,1:T(8,128)(2,1)}, u32[]{:S(2)}) copy-start(bf16[256,256]{0,1:T(8,128)(2,1)} %fusion.19) | copy-start | bytes 393220
Sparse Core Ops, SparseCore 0:
  45.2 44.4 all-gather.4
  93.5 64.4 reduce-scatter.1
  164.4 37.9 all-gather.6
  207.2 106.9 all-reduce.8
  316.4 104.4 all-gather.8
  433.3 103.7 all-reduce.10
  614.1 41.7 all-gather.10
where the time goes:
time: 700 us; the launch traced here: 699 us
  waiting for transfers between devices  466 us (67%)
  other arithmetic  73.8 us (11%)
  blocking collectives  71.5 us (10%)
  matrix products  39.3 us (6%)
  local copies, waits for them, and re-layouts  26.9 us (4%)
  between operations  15.8 us (2%)
    psum x1, waiting for transfers between devices, per_device(): lax.psum(grad_part.astype(jnp.bfloat16), 'dp').astype(jnp.float32)  107 us
    psum x1, waiting for transfers between devices, per_device(): gram_matrix = lax.psum(gram_local, 'fsdp')  103 us
    all_gather x1, waiting for transfers between devices, per_device(): lax.all_gather(right_prev, 'fsdp', axis=0, tiled=True)  94.7 us
    reduce_scatter x1, waiting for transfers between devices, per_device(): lax.psum_scatter(jnp.einsum('cd,ld->cl', weight_rows, cot_cols, preferred...  58.3 us
    all_gather x1, waiting for transfers between devices, per_device(): shard_piece = lax.all_gather(gated_out, 'fsdp', axis=1, tiled=True)  38 us
    another operation x7, other arithmetic, per_device(): lower_factor = jnp.linalg.cholesky(gram_matrix)  36.4 us
    psum x1, blocking collectives, per_device(): square_sums = lax.psum(jnp.sum(x_cols * x_cols, axis=1), 'fsdp')  34.9 us
    all_gather x1, waiting for transfers between devices, per_device(): lax.all_gather(normed_cols, 'fsdp', axis=1, tiled=True)  34.7 us
  transfers between devices with their start and end apart: 8, of which 8 were waited for; matrix products, arithmetic and copies ran while one was open for 6% of the time, Pallas kernels for 0%

commit v1 on v0

--- a/solution.py
+++ b/solution.py
@@ -6,6 +6,12 @@
 D = 8192
 C = 4096
 GROUP = 16
+
+
+def trade_parts(array, mesh_axis, split, join):
+    cells = jnp.split(array, lax.axis_size(mesh_axis), axis=split)
+    received = lax.all_to_all(jnp.stack(cells), mesh_axis, 0, 0)
+    return jnp.concatenate(received, axis=join)
 
 
 def shifted(signal, lag, tap_count):
@@ -109,7 +115,7 @@
         lax.psum(filter_part.astype(jnp.bfloat16), "dp").astype(jnp.float32),
     )
     grad_half = grad_total.astype(jnp.bfloat16)
-    grad_rows_own = lax.all_to_all(grad_half, "fsdp", split_axis=0, concat_axis=1, tiled=True)
+    grad_rows_own = trade_parts(grad_half, "fsdp", 0, 1)
     panel_own = jnp.dot(
         grad_rows_own,
         lax.all_gather(right_prev, "fsdp", axis=0, tiled=True),

time: 700 us -> 729 us (1.041)
  local copies, waits for them, and re-layouts: 26.9 us -> 53.6 us
    all_to_all x1, waiting for transfers between devices: 6.47 us -> 102 us  [trade_parts(): received = lax.all_to_all(jnp.stack(cells), mesh_axis, 0, 0)]
    all_gather x1, waiting for transfers between devices: 94.7 us -> 0.01 us  [per_device(): lax.all_gather(right_prev, 'fsdp', axis=0, tiled=True)]
    unnamed x46 -> x61, local copies, waits for them, and re-layouts: 2.47 us -> 27.5 us
  transfers between devices with their start and end apart: 8 -> 8, of which waited for: 8 -> 7; matrix products, arithmetic and copies ran while one was open for 6% -> 5% of each run, Pallas kernels for 0% -> 0%
where the time goes in v1:
time: 729 us; the launch traced here: 727 us
  waiting for transfers between devices  467 us (64%)
  other arithmetic  73.8 us (10%)
  blocking collectives  71.5 us (10%)
  local copies, waits for them, and re-layouts  53.6 us (7%)
  matrix products  39.3 us (5%)
  between operations  15.8 us (2%)
    psum x1, waiting for transfers between devices, per_device(): lax.psum(grad_part.astype(jnp.bfloat16), 'dp').astype(jnp.float32)  107 us
    all_to_all x1, waiting for transfers between devices, trade_parts(): received = lax.all_to_all(jnp.stack(cells), mesh_axis, 0, 0)  102 us
    psum x1, waiting for transfers between devices, per_device(): gram_matrix = lax.psum(gram_local, 'fsdp')  102 us
    reduce_scatter x1, waiting for transfers between devices, per_device(): lax.psum_scatter(jnp.einsum('cd,ld->cl', weight_rows, cot_cols, preferred...  58.3 us
    all_gather x1, waiting for transfers between devices, per_device(): shard_piece = lax.all_gather(gated_out, 'fsdp', axis=1, tiled=True)  38 us
    another operation x7, other arithmetic, per_device(): lower_factor = jnp.linalg.cholesky(gram_matrix)  36.4 us
    psum x1, blocking collectives, per_device(): square_sums = lax.psum(jnp.sum(x_cols * x_cols, axis=1), 'fsdp')  34.9 us
    all_gather x1, waiting for transfers between devices, per_device(): lax.all_gather(normed_cols, 'fsdp', axis=1, tiled=True)  34.7 us
  transfers between devices with their start and end apart: 8, of which 7 were waited for; matrix products, arithmetic and copies ran while one was open for 5% of the time, Pallas kernels for 0%

profile of v1, /device:TPU:0, one launch (start us, length us, event | category | flops | bytes accessed | tf_op | source)
XLA Modules:
  0.0 727.0 jit_solution(6328092764293613914)
XLA Ops:
  9.3 34.9 %psum.35 = f32[192]{0:T(256)S(1)} all-reduce(f32[192]{0:T(256)S(1)} %get-tuple-element.121), channel_id=1, replica_groups=mesh['dp'=2,'fsdp'=16] {'fsdp'}, use_global_device_ids=true, to_apply=%region_1.0 | all-reduce | flops 192 | bytes 1536 | tf_op jit(solution)/shard_map/psum | solution.py:61
  45.1 5.4 fusion.30
  55.0 34.7 %all-gather.5.cloned.1.call-done = bf16[192,8192]{1,0:T(8,128)(2,1)} async-done(((bf16[192,512]{1,0:T(8,128)(2,1)}), bf16[192,8192]{1,0:T(8,128)(2,1)}) %all-gather.5.cloned.1.call-update) | async-done | bytes 3145744 | tf_op jit(solution)/shard_map/all_gather | solution.py:68
  89.7 9.8 %fusion.6 = bf16[3,192,256]{2,1,0:T(8,128)(2,1)S(1)} fusion(bf16[3,256,8192]{2,1,0:T(8,128)(2,1)} %param.12, bf16[192,8192]{1,0:T(8,128)(2,1)} %all-gather.5.cloned.1.call-done), kind=kOutput, calls=%fused_computation.8 | convolution fusion | flops 2416066560 | bytes 16023552 | tf_op jit(solution)/shard_map/ld,kcd->klc/dot_general | solution.py:66
  99.6 58.3 %reduce-scatter.2.cloned.1.call-done = f32[256,192]{0,1:T(8,128)} async-done(((f32[4096,192]{0,1:T(8,128)}), f32[256,192]{0,1:T(8,128)}) %reduce-scatter.2.cloned.1.call-update) | async-done | bytes 196624 | tf_op jit(solution)/shard_map/reduce_scatter | solution.py:89
  164.3 38.0 %all-gather.7.cloned.1.call-done = bf16[192,4096]{1,0:T(8,128)(2,1)} async-done(((bf16[192,256]{1,0:T(8,128)(2,1)}), bf16[192,4096]{1,0:T(8,128)(2,1)}) %all-gather.7.cloned.1.call-update) | async-done | bytes 1572880 | tf_op jit(solution)/shard_map/all_gather | solution.py:82
  202.3 4.7 convolution_convert_fusion
  207.1 107.1 %all-reduce.9.cloned.1.call-done = bf16[4096,512]{1,0:T(8,128)(2,1)} async-done(((bf16[4096,512]{1,0:T(8,128)(2,1)}), bf16[4096,512]{1,0:T(8,128)(2,1)}) %all-reduce.9.cloned.1.call-update) | async-done | bytes 4194320 | tf_op jit(solution)/shard_map/psum | solution.py:114
  340.9 5.7 all-to-all-start
  347.2 102.3 %all-to-all-done = bf16[16,256,512]{2,1,0:T(8,128)(2,1)} async-done(((bf16[16,256,512]{2,1,0:T(8,128)(2,1)}), bf16[16,256,512]{2,1,0:T(8,128)(2,1)}, u32[]{:S(2)}, u32[]{:S(2)}) %all-to-all-start) | async-done | bytes 4194336 | tf_op jit(solution)/shard_map/all_to_all | solution.py:13
  449.6 6.4 copy.22
  455.9 4.8 convolution_convert_fusion.1
  462.5 102.1 %all-reduce.11.cloned.1.call-done = f32[256,256]{0,1:T(8,128)} async-done(((f32[256,256]{0,1:T(8,128)}), f32[256,256]{0,1:T(8,128)}) %all-reduce.11.cloned.1.call-update) | async-done | bytes 262160 | tf_op jit(solution)/shard_map/psum | solution.py:126
  568.2 11.7 %cholesky.50 = f32[128,128]{1,0:T(8,128)S(1)} custom-call(f32[128,128]{1,0:T(8,128)S(1)} %cholesky.118), custom_call_target="Cholesky" | custom-call | tf_op jit(solution)/shard_map/jit(cholesky)/cholesky | solution.py:127
  581.2 9.8 %custom-call.15 = f32[1,128,128]{1,2,0:T(8,128)S(1)} custom-call(f32[1,128,128]{2,1,0:T(8,128)S(1)} %get-tuple-element.89), custom_call_target="InvertDiagBlocksLowerTriangular" | custom-call | tf_op jit(solution)/shard_map/jit(cholesky)/cholesky | solution.py:127
  593.8 11.7 %cholesky.105 = f32[128,128]{1,0:T(8,128)S(1)} custom-call(f32[128,128]{1,0:T(8,128)S(1)} %convolution_subtract_fusion.1), custom_call_target="Cholesky" | custom-call | tf_op jit(solution)/shard_map/jit(cholesky)/cholesky | solution.py:127
  611.8 6.8 while.1
  612.4 2.9 bitcast_dynamic-update-slice_fusion.2
  618.6 20.5 %custom-call.16 = f32[2,128,128]{1,2,0:T(8,128)S(1)} custom-call(f32[2,128,128]{2,1,0:T(8,128)} %get-tuple-element.11), custom_call_target="InvertDiagBlocksLowerTriangular" | custom-call | tf_op jit(solution)/shard_map/jit(_solve_triangular)/triangular_solve | solution.py:128
  649.8 5.0 psum.36
  655.4 3.8 fusion.9
  660.0 23.5 %all-gather.11.cloned.1.call-done = bf16[4096,256]{0,1:T(8,128)(2,1)} async-done(((bf16[256,256]{0,1:T(8,128)(2,1)}), bf16[4096,256]{0,1:T(8,128)(2,1)}) %all-gather.11.cloned.1.call-update) | async-done | bytes 2097168 | tf_op jit(solution)/shard_map/all_gather | solution.py:135
  683.5 4.2 multiply_reduce_fusion
  687.7 31.6 %psum.39 = f32[256]{0:T(256)S(1)} all-reduce(f32[256]{0:T(256)S(1)} %get-tuple-element.125), channel_id=1, replica_groups=mesh['dp'=2,'fsdp'=16] {'fsdp'}, use_global_device_ids=true, to_apply=%region_43.44 | all-reduce | flops 256 | bytes 2048 | tf_op jit(solution)/shard_map/psum | solution.py:138
  (214 shorter events, 72.2 us)
Async XLA Ops:
  7.2 1.1 copy-start
  7.2 82.5 %all-gather.5.cloned.1.call-start = ((), (), s32[]{:S(2)}) async-start(), calls=%async_computation.2 | async-start | bytes 3342336 | tf_op jit(solution)/shard_map/all_gather | solution.py:68
  45.0 5.5 copy-start.8
  45.0 6.6 copy-start.9
  45.1 112.9 %reduce-scatter.2.cloned.1.call-start = ((), (), s32[]{:S(2)}) async-start(), calls=%async_computation.4 | async-start | bytes 3342336 | tf_op jit(solution)/shard_map/reduce_scatter | solution.py:89
  50.5 151.8 %all-gather.7.cloned.1.call-start = ((), (), s32[]{:S(2)}) async-start(), calls=%async_computation.3 | async-start | bytes 1671168 | tf_op jit(solution)/shard_map/all_gather | solution.py:82
  99.5 102.8 %copy-start.7 = (bf16[1,192,512]{2,1,0:T(8,128)(2,1)S(1)}, bf16[1,192,512]{2,1,0:T(8,128)(2,1)}, u32[]{:S(2)}) copy-start(bf16[1,192,512]{2,1,0:T(8,128)(2,1)} %param.16) | copy-start | bytes 589828
  99.6 61.3 %copy-start.3 = (f32[192,256]{1,0:T(8,128)}, f32[192,256]{1,0:T(8,128)S(1)}, u32[]{:S(2)}) copy-start(f32[192,256]{1,0:T(8,128)S(1)} %get-tuple-element.84) | copy-start | bytes 589828
  159.1 48.0 %copy-start.4 = (f32[192,256]{1,0:T(8,128)}, f32[192,256]{1,0:T(8,128)S(1)}, u32[]{:S(2)}) copy-start(f32[192,256]{1,0:T(8,128)S(1)} %get-tuple-element.79) | copy-start | bytes 589828
  161.0 46.1 %copy-start.2 = (f32[192,256]{1,0:T(8,128)}, f32[192,256]{1,0:T(8,128)S(1)}, u32[]{:S(2)}) copy-start(f32[192,256]{1,0:T(8,128)S(1)} %mul.459) | copy-start | bytes 589828
  164.2 150.0 %all-reduce.9.cloned.1.call-start = ((), (), s32[]{:S(2)}) async-start(), calls=%async_computation.5 | async-start | bytes 8388608 | tf_op jit(solution)/shard_map/psum | solution.py:114
  340.9 108.6 %all-to-all-start = ((bf16[16,256,512]{2,1,0:T(8,128)(2,1)}), bf16[16,256,512]{2,1,0:T(8,128)(2,1)}, u32[]{:S(2)}, u32[]{:S(2)}) async-start(bf16[16,256,512]{2,1,0:T(8,128)(2,1)} %fusion.11), calls=%async_computation.1 | async-start | bytes 8388608 | tf_op jit(solution)/shard_map/all_to_all | solution.py:13
  346.6 109.3 %all-gather.9.cloned.1.call-start = ((), (), s32[]{:S(2)}) async-start(), calls=%async_computation.6 | async-start | bytes 4456448 | tf_op jit(solution)/shard_map/all_gather | solution.py:121
  347.2 217.5 %all-reduce.11.cloned.1.call-start = ((), (), s32[]{:S(2)}) async-start(), calls=%async_computation.7 | async-start | bytes 524288 | tf_op jit(solution)/shard_map/psum | solution.py:126
  461.7 221.9 %all-gather.11.cloned.1.call-start = ((), (), s32[]{:S(2)}) async-start(), calls=%async_computation.8 | async-start | bytes 2228224 | tf_op jit(solution)/shard_map/all_gather | solution.py:135
  462.5 192.9 %copy-start.1 = (bf16[192,4096]{1,0:T(8,128)(2,1)S(1)}, bf16[192,4096]{1,0:T(8,128)(2,1)}, u32[]{:S(2)}) copy-start(bf16[192,4096]{1,0:T(8,128)(2,1)} %all-gather.7.cloned.1.call-done) | copy-start | bytes 4718596
  567.5 0.7 copy-start.6
  644.2 15.0 %copy-start.5 = (bf16[256,256]{0,1:T(8,128)(2,1)S(1)}, bf16[256,256]{0,1:T(8,128)(2,1)}, u32[]{:S(2)}) copy-start(bf16[256,256]{0,1:T(8,128)(2,1)} %fusion.35) | copy-start | bytes 393220
Sparse Core Ops, SparseCore 0:
  45.2 44.4 all-gather.4
  93.5 64.4 reduce-scatter.1
  164.4 37.9 all-gather.6
  207.2 106.9 all-reduce.8
  349.5 94.3 all-gather.8
  461.8 102.8 all-reduce.10
  641.8 41.7 all-gather.10
